TPU v7x, 256 devices: a whole 4x4x8 slice. The times are simulated.
256 devices in a mesh: dp: 16 (over z, core), ctx: 4 (over x), head: 4 (over y).
Axes of the slice: x: 4, y: 4, z: 8, core: 2. Of those that a mesh axis runs over, the one named last changes fastest.
Arguments:
- hidden_in: bfloat16 [16, 2048, 8192], P('dp', 'ctx', 'head'), may hold values from -40 to 40
- w_query: bfloat16 [8192, 4096], P('dp', 'head'), may hold values from -0.0625 to 0.0625
- w_key: bfloat16 [8192, 512], P('dp', 'head'), may hold values from -0.0625 to 0.0625
- w_value: bfloat16 [8192, 512], P('dp', 'head'), may hold values from -0.0625 to 0.0625
- mem_gate: float32 [32], P('head'), may hold values from -3 to 3
Outputs:
- attended: bfloat16 [16, 2048, 4096], P('dp', 'ctx', 'head')
All inputs are finite; a program needn't handle non-finite values.
Results may differ from a plain program's by a relative error of at most 0.011.
Values may be sent and summed in bfloat16 or wider, within the bound.
A program may use at most 128 MiB of HBM per device.

v0:
```python
import math
import jax
import jax.numpy as jnp
from jax import lax
from jax.sharding import PartitionSpec as P

HD = 128
SEG = 128


def entering(shard, axis, combine, identity):
    peers, index = (lax.axis_size(axis), lax.axis_index(axis))
    everything = jax.tree.map(
        lambda part, kind: lax.all_gather(part.astype(kind), axis),
        shard,
        (jnp.bfloat16, jnp.bfloat16),
    )
    start = jax.tree.map(
        lambda part, zero: jnp.broadcast_to(jnp.asarray(zero, part.dtype), part.shape),
        shard,
        identity,
    )

    def lap(k, before):
        reached = k < index
        new = combine(
            before, jax.tree.map(lambda part, own: part[k].astype(own.dtype), everything, shard)
        )
        return jax.tree.map(lambda a, b: jnp.where(reached, a, b), new, before)

    return lax.fori_loop(0, peers, lap, start)


def feature_map(vector):
    return jax.nn.elu(vector) + 1.0


def exclusive_sum(stack):
    running = jnp.cumsum(stack, axis=0)
    return jnp.concatenate([jnp.zeros_like(stack[:1]), running[:-1]], axis=0)


def add_pair(earlier, later):
    return (earlier[0] + later[0], earlier[1] + later[1])


def body(hidden_in, w_query, w_key, w_value, mem_gate):
    highest = lax.Precision.HIGHEST
    features = lax.all_gather(hidden_in, "head", axis=2, tiled=True)
    tok_rows = features.shape[1]
    flattened = features[0]
    query_full = jnp.dot(
        flattened,
        lax.all_gather(w_query, "dp", axis=0, tiled=True),
        preferred_element_type=jnp.float32,
    )
    keys_full = jnp.dot(
        flattened,
        lax.all_gather(w_key, "dp", axis=0, tiled=True),
        preferred_element_type=jnp.float32,
    )
    values_full = jnp.dot(
        flattened,
        lax.all_gather(w_value, "dp", axis=0, tiled=True),
        preferred_element_type=jnp.float32,
    )
    query = query_full.astype(jnp.bfloat16)
    keys = keys_full.astype(jnp.bfloat16)
    values = values_full.astype(jnp.bfloat16)
    heads_dev = query.shape[1] // HD
    kv_dev = keys.shape[1] // HD
    group_size = heads_dev // kv_dev
    segments = tok_rows // SEG
    query_seg = query.reshape(segments, SEG, kv_dev, group_size, HD)
    key_seg = keys.reshape(segments, SEG, kv_dev, HD)
    value_seg = values.reshape(segments, SEG, kv_dev, HD)
    scores = jnp.einsum(
        "nqkgd,nskd->nkgqs", query_seg, key_seg, preferred_element_type=jnp.float32
    ) / math.sqrt(HD)
    causal = jnp.arange(SEG)[:, None] >= jnp.arange(SEG)[None, :]
    scores = jnp.where(causal, scores, -jnp.inf)
    probs = jax.nn.softmax(scores, axis=-1).astype(jnp.bfloat16)
    local = jnp.einsum("nkgqs,nskd->nqkgd", probs, value_seg, preferred_element_type=jnp.float32)
    value_wide = value_seg.astype(jnp.float32)
    feat_key = feature_map(key_seg.astype(jnp.float32))
    increment = jnp.einsum("nskd,nske->nkde", feat_key, value_wide, precision=highest)
    key_mass = jnp.sum(feat_key, axis=1)
    state_total = jnp.sum(increment, axis=0)
    mass_total = jnp.sum(key_mass, axis=0)
    prior_state, prior_mass = entering(
        (state_total, mass_total),
        "ctx",
        add_pair,
        (jnp.zeros_like(state_total), jnp.zeros_like(mass_total)),
    )
    memory = prior_state[None] + exclusive_sum(increment)
    mass_prior = prior_mass[None] + exclusive_sum(key_mass)
    feat_query = feature_map(query_seg.astype(jnp.float32))
    numerator = jnp.einsum("nqkgd,nkde->nqkge", feat_query, memory, precision=highest)
    denominator = jnp.einsum("nqkgd,nkd->nqkg", feat_query, mass_prior, precision=highest) + 1.0
    retrieved = numerator / denominator[..., None]
    gate_share = jax.nn.sigmoid(mem_gate).reshape(kv_dev, group_size)[None, None, :, :, None]
    mixed = gate_share * retrieved + (1.0 - gate_share) * local
    return mixed.reshape(1, tok_rows, heads_dev * HD).astype(jnp.bfloat16)


def solution(mesh):
    return jax.shard_map(
        body,
        mesh=mesh,
        in_specs=(
            P("dp", "ctx", "head"),
            P("dp", "head"),
            P("dp", "head"),
            P("dp", "head"),
            P("head"),
        ),
        out_specs=P("dp", "ctx", "head"),
        check_vma=False,
    )
```

profile of v0, /device:TPU:1, one launch (start us, length us, event | category | flops | bytes accessed | tf_op | source)
XLA Modules:
  0.0 307.1 jit_solution(8610718658696810357)
XLA Ops:
  6.5 0.7 all-gather.12.cloned.1.call-update
  7.3 0.7 all-gather.8.cloned.1.call-update
  8.1 0.7 all-gather.10.cloned.1.call-update
  8.8 0.5 all-gather.14.cloned.1.call-update
  9.4 43.4 %all-gather.12.cloned.1.call-done = bf16[8192,128]{1,0:T(8,128)(2,1)} async-done(((bf16[512,128]{1,0:T(8,128)(2,1)}), bf16[8192,128]{1,0:T(8,128)(2,1)}) %all-gather.12.cloned.1.call-update) | async-done | bytes 2097168 | tf_op jit(solution)/shard_map/all_gather | solution.py:64
  52.8 85.3 %all-gather.8.cloned.1.call-done = bf16[1,512,8192]{2,1,0:T(8,128)(2,1)} async-done(((bf16[1,512,2048]{2,1,0:T(8,128)(2,1)}), bf16[1,512,8192]{2,1,0:T(8,128)(2,1)}) %all-gather.8.cloned.1.call-update) | async-done | bytes 8388624 | tf_op jit(solution)/shard_map/all_gather | solution.py:49
  138.1 6.3 %fusion.24 = bf16[512,128]{1,0:T(8,128)(2,1)S(1)} fusion(bf16[8192,128]{1,0:T(8,128)(2,1)} %all-gather.12.cloned.1.call-done, bf16[1,512,8192]{2,1,0:T(8,128)(2,1)} %all-gather.8.cloned.1.call-done), kind=kOutput, calls=%fused_computation.27 | convolution fusion | flops 1073807360 | bytes 10616832 | tf_op jit(solution)/shard_map/dot_general | solution.py:62
  144.4 36.5 %all-gather.10.cloned.1.call-done = bf16[8192,128]{1,0:T(8,128)(2,1)} async-done(((bf16[512,128]{1,0:T(8,128)(2,1)}), bf16[8192,128]{1,0:T(8,128)(2,1)}) %all-gather.10.cloned.1.call-update) | async-done | bytes 2097168 | tf_op jit(solution)/shard_map/all_gather | solution.py:59
  180.9 6.3 %fusion.42 = (bf16[128]{0:T(256)(128)(2,1)S(1)}, bf16[512,128]{1,0:T(8,128)(2,1)S(1)}) fusion(bf16[8192,128]{1,0:T(8,128)(2,1)} %all-gather.10.cloned.1.call-done, bf16[1,512,8192]{2,1,0:T(8,128)(2,1)} %all-gather.8.cloned.1.call-done), kind=kOutput, calls=%fused_computation.48 | convolution fusion | flops 1074200448 | bytes 10617088 | tf_op jit(solution)/shard_map/dot_general | solution.py:57
  187.3 0.5 fusion.64
  187.7 0.2 fusion.47
  188.1 7.6 %all-gather.2 = bf16[4,1,128]{2,1,0:T(2,128)(2,1)S(1)} all-gather(bf16[1,1,128]{2,1,0:T(2,128)(2,1)S(1)} %bitcast.115), channel_id=3, replica_groups=mesh['dp'=16,'ctx'=4,'head'=4] {'ctx'}, dimensions={0}, use_global_device_ids=true | all-gather | bytes 1280 | tf_op jit(solution)/shard_map/all_gather | solution.py:14
  195.7 10.5 %all-gather = bf16[512,128]{1,0:T(8,128)(2,1)S(1)} all-gather(bf16[128,128]{1,0:T(8,128)(2,1)S(1)} %get-tuple-element.152), channel_id=2, replica_groups=mesh['dp'=16,'ctx'=4,'head'=4] {'ctx'}, dimensions={0}, use_global_device_ids=true | all-gather | bytes 163840 | tf_op jit(solution)/shard_map/all_gather | solution.py:14
  206.2 0.2 while.16
  206.4 70.0 %all-gather.14.cloned.1.call-done = bf16[8192,1024]{1,0:T(8,128)(2,1)} async-done(((bf16[512,1024]{1,0:T(8,128)(2,1)}), bf16[8192,1024]{1,0:T(8,128)(2,1)}) %all-gather.14.cloned.1.call-update) | async-done | bytes 16777232 | tf_op jit(solution)/shard_map/all_gather | solution.py:54
  276.4 14.8 %fusion.18 = bf16[64,8,8,128]{3,1,2,0:T(8,128)(2,1)S(1)} fusion(bf16[8192,1024]{1,0:T(8,128)(2,1)} %all-gather.14.cloned.1.call-done, bf16[1,512,8192]{2,1,0:T(8,128)(2,1)} %all-gather.8.cloned.1.call-done), kind=kOutput, calls=%fused_computation.25 | convolution fusion | flops 8590458880 | bytes 26214400 | tf_op jit(solution)/shard_map/dot_general | solution.py:52
  291.2 0.3 copy.37
  291.5 2.5 fusion.10
  294.1 2.8 fusion.12
  296.9 0.5 fusion.65
  297.3 0.4 fusion.14
  297.7 0.8 fusion.8
  298.5 0.7 copy.25
  299.3 1.3 convert_element_type.134
  (26 shorter events, 0.5 us)
Async XLA Ops:
  6.5 2.8 copy-start.1
  6.5 46.3 %all-gather.12.cloned.1.call-start = ((), (), s32[]{:S(2)}) async-start(), calls=%async_computation.2 | async-start | bytes 2228224 | tf_op jit(solution)/shard_map/all_gather | solution.py:64
  7.3 130.9 %all-gather.8.cloned.1.call-start = ((), (), s32[]{:S(2)}) async-start(), calls=%async_computation | async-start | bytes 10485760 | tf_op jit(solution)/shard_map/all_gather | solution.py:49
  8.0 172.9 %all-gather.10.cloned.1.call-start = ((), (), s32[]{:S(2)}) async-start(), calls=%async_computation.1 | async-start | bytes 2228224 | tf_op jit(solution)/shard_map/all_gather | solution.py:59
  8.7 267.7 %all-gather.14.cloned.1.call-start = ((), (), s32[]{:S(2)}) async-start(), calls=%async_computation.3 | async-start | bytes 17825792 | tf_op jit(solution)/shard_map/all_gather | solution.py:54
  187.9 103.3 %copy-start = (f32[4,1,128,128]{3,2,0,1:T(8,128)}, f32[4,1,128,128]{3,2,0,1:T(8,128)S(1)}, u32[]{:S(2)}) copy-start(f32[4,1,128,128]{3,2,0,1:T(8,128)S(1)} %fusion.47) | copy-start | bytes 786436
  291.5 2.5 slice-start
Sparse Core Ops, SparseCore 0:
  9.2 43.6 all-gather.11
  54.6 83.4 all-gather.7
  139.9 40.9 all-gather.9
  182.6 93.7 all-gather.13
where the time goes:
time: 307 us
  waiting for transfers between devices  238 us (78%)
  matrix products  34.5 us (11%)
  blocking collectives  18.1 us (6%)
  between operations  13.3 us (4%)
    all_gather x1, waiting for transfers between devices, body(): features = lax.all_gather(hidden_in, 'head', axis=2, tiled=True)  85.3 us
    all_gather x1, waiting for transfers between devices, body(): lax.all_gather(w_query, 'dp', axis=0, tiled=True)  70 us
    all_gather x1, waiting for transfers between devices, body(): lax.all_gather(w_value, 'dp', axis=0, tiled=True)  43.4 us
    all_gather x1, waiting for transfers between devices, body(): lax.all_gather(w_key, 'dp', axis=0, tiled=True)  36.5 us
    all_gather x2, blocking collectives, entering(): lax.all_gather(part.astype(kind), axis)  18.1 us
    dot_general x1, matrix products, body(): jnp.dot(flattened, lax.all_gather(w_query, 'dp', axis=0, tiled=True), pre...  14.8 us
    dot_general x1, matrix products, body(): jnp.dot(flattened, lax.all_gather(w_key, 'dp', axis=0, tiled=True), prefe...  6.33 us
    dot_general x1, matrix products, body(): jnp.dot(flattened, lax.all_gather(w_value, 'dp', axis=0, tiled=True), pre...  6.3 us
  transfers between devices with their start and end apart: 4, of which 4 were waited for; matrix products, arithmetic and copies ran while one was open for 4% of the time, Pallas kernels for 0%

commit v1 on v0

--- a/solution.py
+++ b/solution.py
@@ -6,6 +6,27 @@
 
 HD = 128
 SEG = 128
+
+
+def collect(shard, axis, dim):
+    count, place, rows = (lax.axis_size(axis), lax.axis_index(axis), shard.shape[dim])
+    upward = [(i, (i + 1) % count) for i in range(count)]
+    left = [(i, (i - 1) % count) for i in range(count)]
+    filled = jnp.zeros((*shard.shape[:dim], count * rows, *shard.shape[dim + 1 :]), shard.dtype)
+    filled = lax.dynamic_update_slice_in_dim(filled, shard, place * rows, axis=dim)
+    from_left = from_right = shard
+    half = count // 2
+    for hop in range(1, half + 1):
+        from_left = lax.ppermute(from_left, axis, upward)
+        filled = lax.dynamic_update_slice_in_dim(
+            filled, from_left, (place - hop) % count * rows, axis=dim
+        )
+        if hop < count - half:
+            from_right = lax.ppermute(from_right, axis, left)
+            filled = lax.dynamic_update_slice_in_dim(
+                filled, from_right, (place + hop) % count * rows, axis=dim
+            )
+    return filled
 
 
 def entering(shard, axis, combine, identity):
@@ -59,11 +80,7 @@
         lax.all_gather(w_key, "dp", axis=0, tiled=True),
         preferred_element_type=jnp.float32,
     )
-    values_full = jnp.dot(
-        flattened,
-        lax.all_gather(w_value, "dp", axis=0, tiled=True),
-        preferred_element_type=jnp.float32,
-    )
+    values_full = jnp.dot(flattened, collect(w_value, "dp", 0), preferred_element_type=jnp.float32)
     query = query_full.astype(jnp.bfloat16)
     keys = keys_full.astype(jnp.bfloat16)
     values = values_full.astype(jnp.bfloat16)

time: 307 us -> 268 us (0.87)
  waiting for transfers between devices: 238 us -> 166 us
  starting transfers between devices: 0.12 us -> 31 us
    all_gather x1 -> x0, waiting for transfers between devices: 43.4 us -> none  [body(): lax.all_gather(w_value, 'dp', axis=0, tiled=True)]
    all_gather x1, waiting for transfers between devices: 85.3 us -> 45.7 us  [body(): features = lax.all_gather(hidden_in, 'head', axis=2, tiled=True)]
    ppermute x0 -> x15, starting transfers between devices: none -> 30.9 us  [the longest x7 23.6 us: collect(): from_right = lax.ppermute(from_right, axis, left)]
    ppermute x0 -> x15, waiting for transfers between devices: none -> 11.9 us  [the longest x8 9.46 us: collect(): from_left = lax.ppermute(from_left, axis, upward)]
  transfers between devices with their start and end apart: 4 -> 18, of which waited for: 4 -> 18; matrix products, arithmetic and copies ran while one was open for 4% -> 5% of each run, Pallas kernels for 0% -> 0%
where the time goes in v1:
time: 268 us
  waiting for transfers between devices  166 us (62%)
  matrix products  34.4 us (13%)
  starting transfers between devices  31 us (12%)
  blocking collectives  18.1 us (7%)
  between operations  13.7 us (5%)
  local copies, waits for them, and re-layouts  2.94 us (1%)
    all_gather x1, waiting for transfers between devices, body(): lax.all_gather(w_query, 'dp', axis=0, tiled=True)  70.1 us
    all_gather x1, waiting for transfers between devices, body(): features = lax.all_gather(hidden_in, 'head', axis=2, tiled=True)  45.7 us
    all_gather x1, waiting for transfers between devices, body(): lax.all_gather(w_key, 'dp', axis=0, tiled=True)  36.5 us
    ppermute x7, starting transfers between devices, collect(): from_right = lax.ppermute(from_right, axis, left)  23.6 us
    all_gather x2, blocking collectives, entering(): lax.all_gather(part.astype(kind), axis)  18.1 us
    dot_general x1, matrix products, body(): jnp.dot(flattened, lax.all_gather(w_query, 'dp', axis=0, tiled=True), pre...  14.8 us
    ppermute x8, waiting for transfers between devices, collect(): from_left = lax.ppermute(from_left, axis, upward)  9.46 us
    ppermute x8, starting transfers between devices, collect(): from_left = lax.ppermute(from_left, axis, upward)  7.31 us
  transfers between devices with their start and end apart: 18, of which 18 were waited for; matrix products, arithmetic and copies ran while one was open for 5% of the time, Pallas kernels for 0%

profile of v1, /device:TPU:1, one launch (start us, length us, event | category | flops | bytes accessed | tf_op | source)
XLA Modules:
  0.0 267.5 jit_solution(837553691798934247)
XLA Ops:
  8.8 3.0 %collective-permute-start = (bf16[512,128]{1,0:T(8,128)(2,1)S(1)}, bf16[512,128]{1,0:T(8,128)(2,1)S(1)}, u32[]{:S(2)}, u32[]{:S(2)}) collective-permute-start(bf16[512,128]{1,0:T(8,128)(2,1)S(1)} %copy-done.1), channel_id=1, source_target_pairs={{0,16},{16,32},{32,48},{48,64},{64,80},{80,96},{96,112},{112,128},... | collective-permute-start | bytes 393224 | tf_op jit(solution)/shard_map/ppermute | solution.py:20
  12.7 1.0 collective-permute-done
  13.7 2.4 collective-permute-start.2
  16.5 1.7 collective-permute-start.3
  19.1 1.5 collective-permute-start.4
  20.9 3.0 %collective-permute-start.5 = (bf16[512,128]{1,0:T(8,128)(2,1)S(1)}, bf16[512,128]{1,0:T(8,128)(2,1)S(1)}, u32[]{:S(2)}, u32[]{:S(2)}) collective-permute-start(bf16[512,128]{1,0:T(8,128)(2,1)S(1)} %collective-permute-done.3), channel_id=1, source_target_pairs={{0,240},{16,0},{32,16},{48,32},{64,48},{80,64},{96,80},{112,96},{1... | collective-permute-start | bytes 393224 | tf_op jit(solution)/shard_map/ppermute | solution.py:25
  25.3 4.2 %collective-permute-start.7 = (bf16[512,128]{1,0:T(8,128)(2,1)S(1)}, bf16[512,128]{1,0:T(8,128)(2,1)S(1)}, u32[]{:S(2)}, u32[]{:S(2)}) collective-permute-start(bf16[512,128]{1,0:T(8,128)(2,1)S(1)} %collective-permute-done.5), channel_id=1, source_target_pairs={{0,240},{16,0},{32,16},{48,32},{64,48},{80,64},{96,80},{112,96},{1... | collective-permute-start | bytes 393224 | tf_op jit(solution)/shard_map/ppermute | solution.py:25
  30.4 4.6 %collective-permute-start.9 = (bf16[512,128]{1,0:T(8,128)(2,1)S(1)}, bf16[512,128]{1,0:T(8,128)(2,1)S(1)}, u32[]{:S(2)}, u32[]{:S(2)}) collective-permute-start(bf16[512,128]{1,0:T(8,128)(2,1)S(1)} %collective-permute-done.7), channel_id=1, source_target_pairs={{0,240},{16,0},{32,16},{48,32},{64,48},{80,64},{96,80},{112,96},{1... | collective-permute-start | bytes 393224 | tf_op jit(solution)/shard_map/ppermute | solution.py:25
  36.0 4.9 %collective-permute-start.11 = (bf16[512,128]{1,0:T(8,128)(2,1)S(1)}, bf16[512,128]{1,0:T(8,128)(2,1)S(1)}, u32[]{:S(2)}, u32[]{:S(2)}) collective-permute-start(bf16[512,128]{1,0:T(8,128)(2,1)S(1)} %collective-permute-done.9), channel_id=1, source_target_pairs={{0,240},{16,0},{32,16},{48,32},{64,48},{80,64},{96,80},{112,96},{1... | collective-permute-start | bytes 393224 | tf_op jit(solution)/shard_map/ppermute | solution.py:25
  41.9 5.0 %collective-permute-start.13 = (bf16[512,128]{1,0:T(8,128)(2,1)S(1)}, bf16[512,128]{1,0:T(8,128)(2,1)S(1)}, u32[]{:S(2)}, u32[]{:S(2)}) collective-permute-start(bf16[512,128]{1,0:T(8,128)(2,1)S(1)} %collective-permute-done.11), channel_id=1, source_target_pairs={{0,240},{16,0},{32,16},{48,32},{64,48},{80,64},{96,80},{112,96},{1... | collective-permute-start | bytes 393224 | tf_op jit(solution)/shard_map/ppermute | solution.py:25
  47.1 0.8 collective-permute-done.13
  47.9 4.7 %collective-permute-done.14 = bf16[512,128]{1,0:T(8,128)(2,1)S(1)} collective-permute-done((bf16[512,128]{1,0:T(8,128)(2,1)S(1)}, bf16[512,128]{1,0:T(8,128)(2,1)S(1)}, u32[]{:S(2)}, u32[]{:S(2)}) %collective-permute-start.14) | collective-permute-done | bytes 131104 | tf_op jit(solution)/shard_map/ppermute | solution.py:20
  52.7 45.7 %all-gather.7.cloned.1.call-done = bf16[1,512,8192]{2,1,0:T(8,128)(2,1)} async-done(((bf16[1,512,2048]{2,1,0:T(8,128)(2,1)}), bf16[1,512,8192]{2,1,0:T(8,128)(2,1)}) %all-gather.7.cloned.1.call-update) | async-done | bytes 8388624 | tf_op jit(solution)/shard_map/all_gather | solution.py:70
  98.4 6.3 %fusion.24 = bf16[128,512]{1,0:T(8,128)(2,1)S(1)} fusion(bf16[8192,128]{1,0:T(8,128)(2,1)S(1)} %constant_dynamic-update-slice_fusion, bf16[1,512,8192]{2,1,0:T(8,128)(2,1)} %all-gather.7.cloned.1.call-done), kind=kOutput, calls=%fused_computation.27 | convolution fusion | flops 1073807360 | bytes 10616832 | tf_op jit(solution)/shard_map/dot_general | solution.py:83
  104.7 36.5 %all-gather.9.cloned.1.call-done = bf16[8192,128]{1,0:T(8,128)(2,1)} async-done(((bf16[512,128]{1,0:T(8,128)(2,1)}), bf16[8192,128]{1,0:T(8,128)(2,1)}) %all-gather.9.cloned.1.call-update) | async-done | bytes 2097168 | tf_op jit(solution)/shard_map/all_gather | solution.py:80
  141.3 6.3 %fusion.42 = (bf16[128]{0:T(256)(128)(2,1)S(1)}, bf16[512,128]{1,0:T(8,128)(2,1)S(1)}) fusion(bf16[8192,128]{1,0:T(8,128)(2,1)} %all-gather.9.cloned.1.call-done, bf16[1,512,8192]{2,1,0:T(8,128)(2,1)} %all-gather.7.cloned.1.call-done), kind=kOutput, calls=%fused_computation.48 | convolution fusion | flops 1074200448 | bytes 10617088 | tf_op jit(solution)/shard_map/dot_general | solution.py:78
  148.4 7.6 %all-gather.2 = bf16[4,1,128]{2,1,0:T(2,128)(2,1)S(1)} all-gather(bf16[1,1,128]{2,1,0:T(2,128)(2,1)S(1)} %bitcast.123), channel_id=3, replica_groups=mesh['dp'=16,'ctx'=4,'head'=4] {'ctx'}, dimensions={0}, use_global_device_ids=true | all-gather | bytes 1280 | tf_op jit(solution)/shard_map/all_gather | solution.py:35
  156.1 10.5 %all-gather = bf16[512,128]{1,0:T(8,128)(2,1)S(1)} all-gather(bf16[128,128]{1,0:T(8,128)(2,1)S(1)} %get-tuple-element.152), channel_id=2, replica_groups=mesh['dp'=16,'ctx'=4,'head'=4] {'ctx'}, dimensions={0}, use_global_device_ids=true | all-gather | bytes 163840 | tf_op jit(solution)/shard_map/all_gather | solution.py:35
  166.8 70.1 %all-gather.11.cloned.1.call-done = bf16[8192,1024]{1,0:T(8,128)(2,1)} async-done(((bf16[512,1024]{1,0:T(8,128)(2,1)}), bf16[8192,1024]{1,0:T(8,128)(2,1)}) %all-gather.11.cloned.1.call-update) | async-done | bytes 16777232 | tf_op jit(solution)/shard_map/all_gather | solution.py:75
  236.9 14.8 %fusion.18 = bf16[64,8,8,128]{3,1,2,0:T(8,128)(2,1)S(1)} fusion(bf16[8192,1024]{1,0:T(8,128)(2,1)} %all-gather.11.cloned.1.call-done, bf16[1,512,8192]{2,1,0:T(8,128)(2,1)} %all-gather.7.cloned.1.call-done), kind=kOutput, calls=%fused_computation.25 | convolution fusion | flops 8590458880 | bytes 26214400 | tf_op jit(solution)/shard_map/dot_general | solution.py:73
  251.9 2.5 fusion.10
  254.5 2.8 %fusion.12 = f32[4,128,128,8]{2,1,3,0:T(8,128)S(1)} fusion(bf16[4,128,8,128]{3,2,1,0:T(8,128)(2,1)S(1)} %bitcast.111, f32[3,1,128,128]{3,2,0,1:T(8,128)S(1)} %slice-done, f32[128,128]{1,0:T(8,128)S(1)} %bitcast.113), kind=kOutput, calls=%fused_computation.22 | convolution fusion | flops 807993344 | bytes 3407872 | tf_op jit(solution)/shard_map/nqkgd,nkde->nqkge/dot_general | solution.py:116
  258.1 0.8 fusion.8
  259.7 1.3 convert_element_type.138
  (73 shorter events, 11.7 us)
Async XLA Ops:
  6.5 2.2 copy-start.1
  6.5 5.5 %copy-start.2 = (f32[8]{0:T(128)S(1)}, f32[8]{0:T(128)}, u32[]{:S(2)}) copy-start(f32[8]{0:T(128)} %param.11) | copy-start | bytes 100
  6.5 91.9 %all-gather.7.cloned.1.call-start = ((), (), s32[]{:S(2)}) async-start(), calls=%async_computation | async-start | bytes 10485760 | tf_op jit(solution)/shard_map/all_gather | solution.py:70
  7.3 134.0 %all-gather.9.cloned.1.call-start = ((), (), s32[]{:S(2)}) async-start(), calls=%async_computation.1 | async-start | bytes 2228224 | tf_op jit(solution)/shard_map/all_gather | solution.py:80
  8.0 228.9 %all-gather.11.cloned.1.call-start = ((), (), s32[]{:S(2)}) async-start(), calls=%async_computation.2 | async-start | bytes 17825792 | tf_op jit(solution)/shard_map/all_gather | solution.py:75
  8.8 5.0 %collective-permute-start = (bf16[512,128]{1,0:T(8,128)(2,1)S(1)}, bf16[512,128]{1,0:T(8,128)(2,1)S(1)}, u32[]{:S(2)}, u32[]{:S(2)}) collective-permute-start(bf16[512,128]{1,0:T(8,128)(2,1)S(1)} %copy-done.1), channel_id=1, source_target_pairs={{0,16},{16,32},{32,48},{48,64},{64,80},{80,96},{96,112},{112,128},... | collective-permute-start | bytes 393224 | tf_op jit(solution)/shard_map/ppermute | solution.py:20
  11.8 4.7 %collective-permute-start.1 = (bf16[512,128]{1,0:T(8,128)(2,1)S(1)}, bf16[512,128]{1,0:T(8,128)(2,1)S(1)}, u32[]{:S(2)}, u32[]{:S(2)}) collective-permute-start(bf16[512,128]{1,0:T(8,128)(2,1)S(1)} %copy-done.1), channel_id=1, source_target_pairs={{0,240},{16,0},{32,16},{48,32},{64,48},{80,64},{96,80},{112,96},{1... | collective-permute-start | bytes 393224 | tf_op jit(solution)/shard_map/ppermute | solution.py:25
  13.7 5.3 %collective-permute-start.2 = (bf16[512,128]{1,0:T(8,128)(2,1)S(1)}, bf16[512,128]{1,0:T(8,128)(2,1)S(1)}, u32[]{:S(2)}, u32[]{:S(2)}) collective-permute-start(bf16[512,128]{1,0:T(8,128)(2,1)S(1)} %collective-permute-done), channel_id=1, source_target_pairs={{0,16},{16,32},{32,48},{48,64},{64,80},{80,96},{96,112},{112,128},... | collective-permute-start | bytes 393224 | tf_op jit(solution)/shard_map/ppermute | solution.py:20
  16.5 4.4 %collective-permute-start.3 = (bf16[512,128]{1,0:T(8,128)(2,1)S(1)}, bf16[512,128]{1,0:T(8,128)(2,1)S(1)}, u32[]{:S(2)}, u32[]{:S(2)}) collective-permute-start(bf16[512,128]{1,0:T(8,128)(2,1)S(1)} %collective-permute-done.1), channel_id=1, source_target_pairs={{0,240},{16,0},{32,16},{48,32},{64,48},{80,64},{96,80},{112,96},{1... | collective-permute-start | bytes 393224 | tf_op jit(solution)/shard_map/ppermute | solution.py:25
  19.1 5.6 %collective-permute-start.4 = (bf16[512,128]{1,0:T(8,128)(2,1)S(1)}, bf16[512,128]{1,0:T(8,128)(2,1)S(1)}, u32[]{:S(2)}, u32[]{:S(2)}) collective-permute-start(bf16[512,128]{1,0:T(8,128)(2,1)S(1)} %collective-permute-done.2), channel_id=1, source_target_pairs={{0,16},{16,32},{32,48},{48,64},{64,80},{80,96},{96,112},{112,128},... | collective-permute-start | bytes 393224 | tf_op jit(solution)/shard_map/ppermute | solution.py:20
  20.9 4.4 %collective-permute-start.5 = (bf16[512,128]{1,0:T(8,128)(2,1)S(1)}, bf16[512,128]{1,0:T(8,128)(2,1)S(1)}, u32[]{:S(2)}, u32[]{:S(2)}) collective-permute-start(bf16[512,128]{1,0:T(8,128)(2,1)S(1)} %collective-permute-done.3), channel_id=1, source_target_pairs={{0,240},{16,0},{32,16},{48,32},{64,48},{80,64},{96,80},{112,96},{1... | collective-permute-start | bytes 393224 | tf_op jit(solution)/shard_map/ppermute | solution.py:25
  24.7 5.6 %collective-permute-start.6 = (bf16[512,128]{1,0:T(8,128)(2,1)S(1)}, bf16[512,128]{1,0:T(8,128)(2,1)S(1)}, u32[]{:S(2)}, u32[]{:S(2)}) collective-permute-start(bf16[512,128]{1,0:T(8,128)(2,1)S(1)} %collective-permute-done.4), channel_id=1, source_target_pairs={{0,16},{16,32},{32,48},{48,64},{64,80},{80,96},{96,112},{112,128},... | collective-permute-start | bytes 393224 | tf_op jit(solution)/shard_map/ppermute | solution.py:20
  25.3 5.2 %collective-permute-start.7 = (bf16[512,128]{1,0:T(8,128)(2,1)S(1)}, bf16[512,128]{1,0:T(8,128)(2,1)S(1)}, u32[]{:S(2)}, u32[]{:S(2)}) collective-permute-start(bf16[512,128]{1,0:T(8,128)(2,1)S(1)} %collective-permute-done.5), channel_id=1, source_target_pairs={{0,240},{16,0},{32,16},{48,32},{64,48},{80,64},{96,80},{112,96},{1... | collective-permute-start | bytes 393224 | tf_op jit(solution)/shard_map/ppermute | solution.py:25
  30.3 5.6 %collective-permute-start.8 = (bf16[512,128]{1,0:T(8,128)(2,1)S(1)}, bf16[512,128]{1,0:T(8,128)(2,1)S(1)}, u32[]{:S(2)}, u32[]{:S(2)}) collective-permute-start(bf16[512,128]{1,0:T(8,128)(2,1)S(1)} %collective-permute-done.6), channel_id=1, source_target_pairs={{0,16},{16,32},{32,48},{48,64},{64,80},{80,96},{96,112},{112,128},... | collective-permute-start | bytes 393224 | tf_op jit(solution)/shard_map/ppermute | solution.py:20
  30.4 5.6 %collective-permute-start.9 = (bf16[512,128]{1,0:T(8,128)(2,1)S(1)}, bf16[512,128]{1,0:T(8,128)(2,1)S(1)}, u32[]{:S(2)}, u32[]{:S(2)}) collective-permute-start(bf16[512,128]{1,0:T(8,128)(2,1)S(1)} %collective-permute-done.7), channel_id=1, source_target_pairs={{0,240},{16,0},{32,16},{48,32},{64,48},{80,64},{96,80},{112,96},{1... | collective-permute-start | bytes 393224 | tf_op jit(solution)/shard_map/ppermute | solution.py:25
  35.9 5.6 %collective-permute-start.10 = (bf16[512,128]{1,0:T(8,128)(2,1)S(1)}, bf16[512,128]{1,0:T(8,128)(2,1)S(1)}, u32[]{:S(2)}, u32[]{:S(2)}) collective-permute-start(bf16[512,128]{1,0:T(8,128)(2,1)S(1)} %collective-permute-done.8), channel_id=1, source_target_pairs={{0,16},{16,32},{32,48},{48,64},{64,80},{80,96},{96,112},{112,128},... | collective-permute-start | bytes 393224 | tf_op jit(solution)/shard_map/ppermute | solution.py:20
  36.0 5.9 %collective-permute-start.11 = (bf16[512,128]{1,0:T(8,128)(2,1)S(1)}, bf16[512,128]{1,0:T(8,128)(2,1)S(1)}, u32[]{:S(2)}, u32[]{:S(2)}) collective-permute-start(bf16[512,128]{1,0:T(8,128)(2,1)S(1)} %collective-permute-done.9), channel_id=1, source_target_pairs={{0,240},{16,0},{32,16},{48,32},{64,48},{80,64},{96,80},{112,96},{1... | collective-permute-start | bytes 393224 | tf_op jit(solution)/shard_map/ppermute | solution.py:25
  41.5 5.6 %collective-permute-start.12 = (bf16[512,128]{1,0:T(8,128)(2,1)S(1)}, bf16[512,128]{1,0:T(8,128)(2,1)S(1)}, u32[]{:S(2)}, u32[]{:S(2)}) collective-permute-start(bf16[512,128]{1,0:T(8,128)(2,1)S(1)} %collective-permute-done.10), channel_id=1, source_target_pairs={{0,16},{16,32},{32,48},{48,64},{64,80},{80,96},{96,112},{112,128},... | collective-permute-start | bytes 393224 | tf_op jit(solution)/shard_map/ppermute | solution.py:20
  41.9 6.0 %collective-permute-start.13 = (bf16[512,128]{1,0:T(8,128)(2,1)S(1)}, bf16[512,128]{1,0:T(8,128)(2,1)S(1)}, u32[]{:S(2)}, u32[]{:S(2)}) collective-permute-start(bf16[512,128]{1,0:T(8,128)(2,1)S(1)} %collective-permute-done.11), channel_id=1, source_target_pairs={{0,240},{16,0},{32,16},{48,32},{64,48},{80,64},{96,80},{112,96},{1... | collective-permute-start | bytes 393224 | tf_op jit(solution)/shard_map/ppermute | solution.py:25
  47.1 5.6 %collective-permute-start.14 = (bf16[512,128]{1,0:T(8,128)(2,1)S(1)}, bf16[512,128]{1,0:T(8,128)(2,1)S(1)}, u32[]{:S(2)}, u32[]{:S(2)}) collective-permute-start(bf16[512,128]{1,0:T(8,128)(2,1)S(1)} %collective-permute-done.12), channel_id=1, source_target_pairs={{0,16},{16,32},{32,48},{48,64},{64,80},{80,96},{96,112},{112,128},... | collective-permute-start | bytes 393224 | tf_op jit(solution)/shard_map/ppermute | solution.py:20
  148.2 103.4 %copy-start = (f32[4,1,128,128]{3,2,0,1:T(8,128)}, f32[4,1,128,128]{3,2,0,1:T(8,128)S(1)}, u32[]{:S(2)}) copy-start(f32[4,1,128,128]{3,2,0,1:T(8,128)S(1)} %fusion.47) | copy-start | bytes 786436
  251.9 2.5 slice-start
Sparse Core Ops, SparseCore 0:
  9.1 89.2 all-gather.6
  100.3 40.9 all-gather.8
  143.1 93.7 all-gather.10
